TPU v7x, 128 devices: a whole 4x4x4 slice. The times are simulated.
128 devices in a mesh: grp: 4 (over y_hi, core), req: 32 (over x, z, y_lo).
Axes of the slice: x: 4, y: 4 (y_hi: 2, y_lo: 2; y = y_hi * 2 + y_lo), z: 4, core: 2. Of those that a mesh axis runs over, the one named last changes fastest.
Arguments:
- tokens: bfloat16 [16384, 1024], P(('grp', 'req')), may hold values from -6 to 6
- attn_gain: float32 [1024], replicated, may hold values from 0.1 to 1.9
- w_query: bfloat16 [1024, 1024], replicated, may hold values from -0.0234375 to 0.0234375
- w_key: bfloat16 [1024, 1024], replicated, may hold values from -0.1875 to 0.1875
- w_value: bfloat16 [1024, 1024], replicated, may hold values from -0.1875 to 0.1875
- w_attn_out: bfloat16 [1024, 1024], replicated, may hold values from -0.1875 to 0.1875
- rel_bias: float32 [32, 16], replicated, may hold values from -4 to 4
- prefix_cache: bfloat16 [8, 512, 2048], P('grp', 'req'), may hold values from -6 to 6
- lengths: int32 [4, 64], P('grp'), may hold values from 1 to 128, 4096 in all within a row
- prefix_map: int32 [4, 64], P('grp'), may hold values from 0 to 1
- mlp_gain: float32 [1024], replicated, may hold values from 0.1 to 1.9
- w_in: bfloat16 [4096, 1024], P('grp'), may hold values from -0.1875 to 0.1875
- w_out: bfloat16 [4096, 1024], P('grp'), may hold values from -0.09375 to 0.09375
Outputs:
- layer_out: bfloat16 [16384, 1024], P(('grp', 'req'))
Inputs may be any that keep to these rules, and one draw needn't show every extreme that they name: In each group the lengths sum to 4096 and the longest is exactly 128.
All inputs are finite; a program needn't handle non-finite values.
Results may differ from a plain program's by a relative error of at most 0.017.
Values may be sent and summed in bfloat16 or wider, within the bound.
No kernel may reach another device: no remote copies, remote signals or barrier semaphores. Data moves between devices by JAX's collectives and lax.ppermute only.
A program may use at most 128 MiB of HBM per device.

v0:
```python
import jax
import jax.numpy as jnp
from jax import lax
from jax.sharding import PartitionSpec as P

D = 1024
H = 16
DK = 64
PLEN = 512
PREF_GRP = 2
epsilon = 1e-06
far_marks = (12, 16, 23, 32, 46, 64, 91)
masked_score = -1e30


def padded(value, sides, width):
    for axis, dim in sides:
        count, length = (lax.axis_size(axis), value.shape[dim])
        up = [(i, (i + 1) % count) for i in range(count - 1)]
        down = [(j, i) for i, j in up]
        last = lax.slice_in_dim(value, length - width, length, axis=dim)
        leading = lax.slice_in_dim(value, 0, width, axis=dim)
        before = lax.ppermute(last, axis, up)
        after = lax.ppermute(leading, axis, down)
        value = jnp.concatenate([before, value, after], axis=dim)
    return value


def bucket_of(relative):
    distance = jnp.abs(relative)
    far_bucket = 8 + sum([(distance >= threshold).astype(jnp.int32) for threshold in far_marks])
    bucket = jnp.where(distance < 8, distance, far_bucket)
    return bucket + jnp.where(relative > 0, 16, 0)


def bias_lookup(relative, rel_bias):
    buckets = bucket_of(relative)
    marks = jnp.arange(rel_bias.shape[0], dtype=jnp.int32)
    one_hot = (buckets[:, :, None] == marks[None, None, :]).astype(jnp.float32)
    return jnp.einsum(
        "qkb,bh->hqk",
        one_hot,
        rel_bias,
        precision=lax.Precision.HIGHEST,
        preferred_element_type=jnp.float32,
    )


def norm_rows(values_in, gain):
    widened = values_in.astype(jnp.float32)
    scale = lax.rsqrt(jnp.mean(widened * widened, axis=-1, keepdims=True) + epsilon)
    return (widened * scale * gain).astype(jnp.bfloat16)


def layout(lengths_row, prefix_row, row_ids):
    req_ends = jnp.cumsum(lengths_row)
    req_starts = req_ends - lengths_row
    member = (
        (row_ids[:, None] >= req_starts[None, :]) & (row_ids[:, None] < req_ends[None, :])
    ).astype(jnp.int32)
    numbers = jnp.arange(lengths_row.shape[0], dtype=jnp.int32)
    req_index = jnp.sum(member * numbers[None, :], axis=1) + jnp.sum(member, axis=1) - 1
    offset = row_ids - jnp.sum(member * req_starts[None, :], axis=1)
    chosen = jnp.sum(member * prefix_row[None, :], axis=1)
    return (req_index, offset, chosen)


def softmax_part(scores, value_rows, allowed):
    scores = jnp.where(allowed[None], scores, masked_score)
    row_max = jnp.max(scores, axis=2)
    exp_terms = jnp.where(allowed[None], jnp.exp(scores - row_max[:, :, None]), 0.0)
    row_sum = jnp.sum(exp_terms, axis=2)
    weighted = jnp.einsum(
        "hqk,khd->hqd",
        exp_terms.astype(jnp.bfloat16),
        value_rows,
        preferred_element_type=jnp.float32,
    )
    return (row_max, row_sum, weighted)


def combine(first_part, second_part):
    row_max = jnp.maximum(first_part[0], second_part[0])
    scale_one = jnp.exp(first_part[0] - row_max)
    scale_two = jnp.exp(second_part[0] - row_max)
    row_sum = first_part[1] * scale_one + second_part[1] * scale_two
    weighted = first_part[2] * scale_one[:, :, None] + second_part[2] * scale_two[:, :, None]
    return (row_max, row_sum, weighted)


def feed_forward(rows_in, in_part, out_part):
    units = lax.dot_general(
        rows_in, in_part, (((1,), (1,)), ((), ())), preferred_element_type=jnp.float32
    )
    units = jnp.maximum(units, 0.0).astype(jnp.bfloat16)
    return jnp.dot(units, out_part, preferred_element_type=jnp.float32)


def body(
    tokens,
    attn_gain,
    w_query,
    w_key,
    w_value,
    w_attn_out,
    rel_bias,
    prefix_cache,
    lengths,
    prefix_map,
    mlp_gain,
    w_in,
    w_out,
):
    rows_here = tokens.shape[0]
    device_pos = lax.axis_index("req")
    group_lengths = lengths[0]
    group_map = prefix_map[0]
    normed = norm_rows(tokens, attn_gain)
    query = (
        jnp.dot(normed, w_query, preferred_element_type=jnp.float32)
        .astype(jnp.bfloat16)
        .reshape(rows_here, H, DK)
    )
    key_value = jnp.concatenate(
        [
            jnp.dot(normed, w_key, preferred_element_type=jnp.float32).astype(jnp.bfloat16),
            jnp.dot(normed, w_value, preferred_element_type=jnp.float32).astype(jnp.bfloat16),
        ],
        axis=1,
    )
    query_ids = device_pos * rows_here + jnp.arange(rows_here, dtype=jnp.int32)
    query_req, query_offset, query_prefix = layout(group_lengths, group_map, query_ids)
    all_positions = jnp.arange(PLEN, dtype=jnp.int32)
    prefix_bias = bias_lookup(all_positions[None, :] - PLEN - query_offset[:, None], rel_bias)
    empty_state = (
        jnp.full((H, rows_here), masked_score, jnp.float32),
        jnp.zeros((H, rows_here), jnp.float32),
        jnp.zeros((H, rows_here, DK), jnp.float32),
    )
    running = empty_state
    shard_kv = lax.all_gather(prefix_cache, "req", axis=1, tiled=True)
    prefix_ids = jnp.arange(PREF_GRP, dtype=jnp.int32)
    slices = shard_kv.shape[0]
    piece_len = shard_kv.shape[1]
    step_len = max(min(piece_len, 512 // slices), 1)
    for begin in range(0, piece_len, step_len):
        width = min(step_len, piece_len - begin)
        block = shard_kv[:, begin : begin + width]
        key_rows = block[:, :, :D].reshape(slices, width, H, DK)
        value_rows = block[:, :, D:].reshape(-1, H, DK)
        rel_terms = lax.dynamic_slice_in_dim(prefix_bias, begin, width, 2)
        prefix_scores = jnp.einsum(
            "qhd,swhd->hqsw", query, key_rows, preferred_element_type=jnp.float32
        )
        prefix_scores = (prefix_scores + rel_terms[:, :, None, :]).reshape(
            H, rows_here, slices * width
        )
        allowed = jnp.repeat(query_prefix[:, None] == prefix_ids[None, :], width, axis=1)
        running = combine(running, softmax_part(prefix_scores, value_rows, allowed))
    state = running
    window = padded(key_value, (("req", 0),), rows_here)
    window_ids = device_pos * rows_here - rows_here + jnp.arange(3 * rows_here, dtype=jnp.int32)
    window_req = layout(group_lengths, group_map, window_ids)[0]
    for part_idx in range(3):
        part_rows = window[part_idx * rows_here : (part_idx + 1) * rows_here]
        part_ids = window_ids[part_idx * rows_here : (part_idx + 1) * rows_here]
        part_req = window_req[part_idx * rows_here : (part_idx + 1) * rows_here]
        suffix_terms = bias_lookup(part_ids[None, :] - query_ids[:, None], rel_bias)
        suffix_allowed = part_req[None, :] == query_req[:, None]
        scores = (
            jnp.einsum(
                "qhd,khd->hqk",
                query,
                part_rows[:, :D].reshape(-1, H, DK),
                preferred_element_type=jnp.float32,
            )
            + suffix_terms
        )
        suffix_state = softmax_part(scores, part_rows[:, D:].reshape(-1, H, DK), suffix_allowed)
        state = combine(state, suffix_state)
    attended = (
        (state[2] / state[1][:, :, None])
        .transpose(1, 0, 2)
        .reshape(rows_here, D)
        .astype(jnp.bfloat16)
    )
    hidden_one = (
        tokens.astype(jnp.float32)
        + jnp.dot(attended, w_attn_out, preferred_element_type=jnp.float32)
    ).astype(jnp.bfloat16)
    normed_two = norm_rows(hidden_one, mlp_gain)
    gathered = lax.all_gather(normed_two, "grp", axis=0, tiled=True)
    mlp_total = lax.psum_scatter(
        feed_forward(gathered, w_in, w_out).astype(jnp.bfloat16),
        "grp",
        scatter_dimension=0,
        tiled=True,
    ).astype(jnp.float32)
    return (hidden_one.astype(jnp.float32) + mlp_total).astype(jnp.bfloat16)


def solution(mesh):
    return jax.shard_map(
        body,
        mesh=mesh,
        in_specs=(
            P(("grp", "req"), None),
            P(),
            P(),
            P(),
            P(),
            P(),
            P(),
            P("grp", "req", None),
            P("grp", None),
            P("grp", None),
            P(),
            P("grp", None),
            P("grp", None),
        ),
        out_specs=P(("grp", "req"), None),
        check_vma=False,
    )
```

profile of v0, /device:TPU:1, one launch (start us, length us, event | category | flops | bytes accessed | tf_op | source)
XLA Modules:
  0.0 308.1 jit_solution(4124527477737952821)
XLA Ops:
  6.5 1.8 copy.91
  8.5 1.2 fusion.46
  9.7 2.2 convolution_convert_fusion.1
  12.0 0.5 convolution_convert_fusion.2
  12.5 0.2 copy-done.12
  12.7 0.8 pad_maximum_fusion
  13.5 1.4 collective-permute-start.1
  14.9 5.5 %collective-permute-start = (bf16[128,2048]{1,0:T(8,128)(2,1)}, bf16[128,2048]{1,0:T(8,128)(2,1)}, u32[]{:S(2)}, u32[]{:S(2)}) collective-permute-start(bf16[128,2048]{1,0:T(8,128)(2,1)} %pad_maximum_fusion), channel_id=1, source_target_pairs={{0,1},{1,2},{2,3},{3,4},{4,5},{5,6},{6,7},{7,8},{8,9},{9,10},{10,1... | collective-permute-start | bytes 1572872 | tf_op jit(solution)/shard_map/ppermute | solution.py:23
  20.4 0.8 copy.108
  21.2 2.1 convolution_convert_fusion.3
  23.8 0.9 fusion.90
  24.7 0.7 fusion.12
  25.5 1.4 copy.109
  27.3 0.3 fusion.68
  27.6 2.6 fusion.13
  30.2 1.3 fusion.137
  31.5 3.0 fusion.10
  34.5 2.7 fusion.131
  37.2 1.8 fusion.11
  39.2 1.8 copy.110
  41.0 2.6 copy.113
  43.6 4.1 %copy.94 = f32[16,128,256]{2,1,0:T(8,128)} copy(f32[16,128,256]{2,0,1:T(8,128)} %get-tuple-element.28) | data formatting | bytes 4194304 | tf_op jit(solution)/shard_map/dynamic_slice | solution.py:151
  47.7 2.5 copy.105
  50.3 4.2 %copy.100 = f32[16,128,256]{2,1,0:T(8,128)} copy(f32[16,128,256]{2,0,1:T(8,128)} %get-tuple-element.29) | data formatting | bytes 4194304 | tf_op jit(solution)/shard_map/dynamic_slice | solution.py:151
  54.4 1.8 fusion.133
  56.3 1.8 copy.114
  58.1 1.8 copy.112
  59.9 1.8 fusion.132
  61.7 1.8 copy.104
  63.5 1.8 copy.106
  65.3 2.0 fusion.136
  67.3 1.0 copy-done.3
  68.5 0.4 fusion.138
  68.8 1.0 copy-done.7
  70.1 97.0 %all-gather.3.cloned.1.call-done = bf16[2,512,2048]{2,0,1:T(2,128)(2,1)} async-done(((bf16[2,16,2048]{2,0,1:T(2,128)(2,1)}), bf16[2,512,2048]{2,0,1:T(2,128)(2,1)}) %all-gather.3.cloned.1.call-update) | async-done | bytes 4194320 | tf_op jit(solution)/shard_map/all_gather | solution.py:141
  167.1 5.7 %fusion.130 = (bf16[2,256,1024]{2,0,1:T(2,128)(2,1)}, bf16[2,256,1024]{2,0,1:T(2,128)(2,1)}, bf16[2,256,1024]{2,0,1:T(2,128)(2,1)}, bf16[2,256,1024]{2,0,1:T(2,128)(2,1)}) fusion(bf16[2,512,2048]{2,0,1:T(2,128)(2,1)} %all-gather.3.cloned.1.call-done), kind=kLoop, calls=%fused_computation.203 | loop fusion | bytes 8388608 | tf_op jit(solution)/shard_map/slice | solution.py:150
  172.8 3.6 %copy.122 = bf16[2,256,1024]{1,2,0:T(8,128)(2,1)} copy(bf16[2,256,1024]{2,0,1:T(2,128)(2,1)} %get-tuple-element.25) | data formatting | bytes 2097152
  176.4 3.7 %copy.123 = bf16[2,256,1024]{1,2,0:T(8,128)(2,1)} copy(bf16[2,256,1024]{2,0,1:T(2,128)(2,1)} %get-tuple-element.27) | data formatting | bytes 2097152
  180.1 2.9 select_reduce_fusion.3
  183.0 2.4 select_reduce_fusion.1
  185.5 2.0 copy-done.2
  187.4 1.2 select_reduce_fusion
  188.7 5.3 %copy.101 = f32[16,128,2,256]{1,3,2,0:T(8,128)} copy(f32[16,128,2,256]{3,1,2,0:T(8,128)} %copy-done.2) | data formatting | bytes 8388608 | tf_op jit(solution)/shard_map/add | solution.py:155
  194.0 5.3 %copy.95 = f32[16,128,2,256]{1,3,2,0:T(8,128)} copy(f32[16,128,2,256]{3,1,2,0:T(8,128)} %copy-done.1) | data formatting | bytes 8388608 | tf_op jit(solution)/shard_map/add | solution.py:155
  199.3 4.9 %copy.96 = bf16[2,256,1024]{1,0,2:T(2,128)(2,1)} copy(bf16[2,256,1024]{2,0,1:T(2,128)(2,1)} %get-tuple-element.26) | data formatting | bytes 2097152 | tf_op jit(solution)/shard_map/slice | solution.py:150
  204.2 2.6 reshape.536
  206.8 4.9 %copy.102 = bf16[2,256,1024]{1,0,2:T(2,128)(2,1)} copy(bf16[2,256,1024]{2,0,1:T(2,128)(2,1)} %get-tuple-element.24) | data formatting | bytes 2097152 | tf_op jit(solution)/shard_map/slice | solution.py:150
  211.6 2.6 reshape.539
  214.2 0.7 fusion.94
  214.9 1.6 fusion.31
  216.5 0.3 fusion.30
  216.9 5.3 %fusion.4 = (bf16[16,128,512]{1,2,0:T(8,128)(2,1)S(1)}, bf16[16,128,512]{1,2,0:T(8,128)(2,1)S(1)}) fusion(f32[16,128,2,256]{1,3,2,0:T(8,128)} %copy.101, f32[16,128]{1,0:T(8,128)S(1)} %get-tuple-element.12, pred[128,512]{0,1:T(8,128)(4,1)S(1)} %bitcast.222, f32[16,128]{1,0:T(8,128)S(1)} %get-tuple-element.61, f32[16,128,2,256]{1,3,2,0:T(8,128)} %copy.95), kind=kLoop, calls=%fused_computation.6 | loop fusion | flops 8388608 | bytes 12664832 | tf_op jit(solution)/shard_map/convert_element_type | solution.py:75
  222.2 0.5 fusion.21
  222.8 0.7 copy-done.11
  223.4 0.5 fusion.22
  224.0 0.7 copy-done.8
  224.7 0.3 fusion.32
  225.0 0.7 copy-done.14
  225.7 0.5 multiply_reduce_fusion
  226.3 0.8 multiply_convert_fusion
  227.2 36.3 %all-gather.5.cloned.1.call-done = bf16[512,1024]{1,0:T(8,128)(2,1)} async-done(((bf16[128,1024]{1,0:T(8,128)(2,1)}), bf16[512,1024]{1,0:T(8,128)(2,1)}) %all-gather.5.cloned.1.call-update) | async-done | bytes 1048592 | tf_op jit(solution)/shard_map/all_gather | solution.py:192
  263.6 5.3 %convolution_convert_fusion = bf16[512,1024]{1,0:T(8,128)(2,1)} fusion(bf16[1024,1024]{1,0:T(8,128)(2,1)S(1)} %copy-done, bf16[512,1024]{1,0:T(8,128)(2,1)} %all-gather.5.cloned.1.call-done, bf16[1024,1024]{1,0:T(8,128)(2,1)} %param.24), kind=kOutput, calls=%fused_computation.27 | convolution fusion | flops 2149056512 | bytes 6291456 | tf_op jit(solution)/shard_map/dot_general | solution.py:96
  268.9 31.0 %reduce-scatter.2.cloned.1.call-done = bf16[128,1024]{1,0:T(8,128)(2,1)} async-done(((bf16[512,1024]{1,0:T(8,128)(2,1)}), bf16[128,1024]{1,0:T(8,128)(2,1)}) %reduce-scatter.2.cloned.1.call-update) | async-done | bytes 262160 | tf_op jit(solution)/shard_map/reduce_scatter | solution.py:193
  299.8 1.7 add_convert_fusion
  (78 shorter events, 1.8 us)
Async XLA Ops:
  6.5 257.0 %copy-start = (bf16[1024,1024]{1,0:T(8,128)(2,1)S(1)}, bf16[1024,1024]{1,0:T(8,128)(2,1)}, u32[]{:S(2)}) copy-start(bf16[1024,1024]{1,0:T(8,128)(2,1)} %param.25) | copy-start | bytes 6291460
  6.5 5.4 %copy-start.4 = (bf16[128,1024]{1,0:T(8,128)(2,1)S(1)}, bf16[128,1024]{1,0:T(8,128)(2,1)}, u32[]{:S(2)}) copy-start(bf16[128,1024]{1,0:T(8,128)(2,1)} %param.13) | copy-start | bytes 786436
  6.5 5.4 %copy-start.21 = (f32[1024]{0:T(1024)S(1)}, f32[1024]{0:T(1024)}, u32[]{:S(2)}) copy-start(f32[1024]{0:T(1024)} %param.14) | copy-start | bytes 12292
  6.5 160.6 %all-gather.3.cloned.1.call-start = ((), (), s32[]{:S(2)}) async-start(), calls=%async_computation.1 | async-start | bytes 4325376 | tf_op jit(solution)/shard_map/all_gather | solution.py:141
  8.4 255.2 %all-gather.5.cloned.1.call-start = ((), (), s32[]{:S(2)}) async-start(), calls=%async_computation.2 | async-start | bytes 1310720 | tf_op jit(solution)/shard_map/all_gather | solution.py:192
  8.5 3.5 %copy-start.13 = (bf16[1024,1024]{1,0:T(8,128)(2,1)S(1)}, bf16[1024,1024]{1,0:T(8,128)(2,1)}, u32[]{:S(2)}) copy-start(bf16[1024,1024]{1,0:T(8,128)(2,1)} %param.16) | copy-start | bytes 6291460
  11.9 0.7 copy-start.12
  13.5 10.0 %copy-start.25 = (s32[1,64]{1,0:T(1,128)S(1)}, s32[1,64]{1,0:T(1,128)}, u32[]{:S(2)}) copy-start(s32[1,64]{1,0:T(1,128)} %param.21) | copy-start | bytes 772
  13.5 11.2 %copy-start.20 = (f32[32,16]{0,1:T(8,128)S(1)}, f32[32,16]{0,1:T(8,128)}, u32[]{:S(2)}) copy-start(f32[32,16]{0,1:T(8,128)} %param.19) | copy-start | bytes 6148
  13.5 40.9 %collective-permute-start.1 = (bf16[128,2048]{1,0:T(8,128)(2,1)}, bf16[128,2048]{1,0:T(8,128)(2,1)}, u32[]{:S(2)}, u32[]{:S(2)}) collective-permute-start(bf16[128,2048]{1,0:T(8,128)(2,1)} %pad_maximum_fusion), channel_id=1, source_target_pairs={{1,0},{2,1},{3,2},{4,3},{5,4},{6,5},{7,6},{8,7},{9,8},{10,9},{11,1... | collective-permute-start | bytes 1572872 | tf_op jit(solution)/shard_map/ppermute | solution.py:24
  14.9 45.0 %collective-permute-start = (bf16[128,2048]{1,0:T(8,128)(2,1)}, bf16[128,2048]{1,0:T(8,128)(2,1)}, u32[]{:S(2)}, u32[]{:S(2)}) collective-permute-start(bf16[128,2048]{1,0:T(8,128)(2,1)} %pad_maximum_fusion), channel_id=1, source_target_pairs={{0,1},{1,2},{2,3},{3,4},{4,5},{5,6},{6,7},{7,8},{8,9},{9,10},{10,1... | collective-permute-start | bytes 1572872 | tf_op jit(solution)/shard_map/ppermute | solution.py:23
  23.3 3.6 %copy-start.26 = (s32[1,64]{1,0:T(1,128)S(1)}, s32[1,64]{1,0:T(1,128)}, u32[]{:S(2)}) copy-start(s32[1,64]{1,0:T(1,128)} %param.22) | copy-start | bytes 772
  26.9 3.3 %copy-start.9 = (f32[128,128,16]{0,1,2:T(8,128)S(1)}, f32[128,128,16]{0,1,2:T(8,128)}, u32[]{:S(2)}) copy-start(f32[128,128,16]{0,1,2:T(8,128)} %copy.109) | copy-start | bytes 3145732
  54.4 131.1 %copy-start.22 = (pred[128,2]{0,1:T(4,128)(4,1)}, pred[128,2]{0,1:T(4,128)(4,1)S(1)}, u32[]{:S(2)}) copy-start(pred[128,2]{0,1:T(4,128)(4,1)S(1)} %iota_compare_fusion.10) | copy-start | bytes 772
  65.3 3.2 %copy-start.10 = (f32[128,128,16]{0,1,2:T(8,128)S(1)}, f32[128,128,16]{0,1,2:T(8,128)}, u32[]{:S(2)}) copy-start(f32[128,128,16]{0,1,2:T(8,128)} %copy.105) | copy-start | bytes 3145732
  65.3 3.2 %copy-start.17 = (bf16[128,1024]{0,1:T(8,128)(2,1)S(1)}, bf16[128,1024]{0,1:T(8,128)(2,1)}, u32[]{:S(2)}) copy-start(bf16[128,1024]{0,1:T(8,128)(2,1)} %copy.104) | copy-start | bytes 786436
  67.3 1.0 copy-start.3
  68.8 1.1 copy-start.7
  180.1 2.9 copy-start.15
  180.1 2.9 copy-start.18
  183.0 2.5 copy-start.1
  185.5 2.0 copy-start.2
  211.6 4.9 %copy-start.16 = (bf16[128,1024]{0,1:T(8,128)(2,1)S(1)}, bf16[128,1024]{0,1:T(8,128)(2,1)}, u32[]{:S(2)}) copy-start(bf16[128,1024]{0,1:T(8,128)(2,1)} %copy.110) | copy-start | bytes 786436
  214.2 2.6 copy-start.23
  216.8 5.4 %copy-start.6 = (bf16[512,16,64]{0,2,1:T(8,128)(2,1)S(1)}, bf16[512,16,64]{0,2,1:T(8,128)(2,1)}, u32[]{:S(2)}) copy-start(bf16[512,16,64]{0,2,1:T(8,128)(2,1)} %reshape.536) | copy-start | bytes 3145732
  222.2 1.2 copy-start.11
  223.4 1.2 copy-start.8
  223.4 1.3 copy-start.19
  224.0 1.1 copy-start.5
  224.0 1.8 copy-start.14
  225.0 1.3 copy-start.24
  227.2 72.7 %reduce-scatter.2.cloned.1.call-start = ((), (), s32[]{:S(2)}) async-start(), calls=%async_computation.3 | async-start | bytes 1310720 | tf_op jit(solution)/shard_map/reduce_scatter | solution.py:193
Sparse Core Ops, SparseCore 0:
  9.0 158.0 all-gather.2
  227.3 36.2 all-gather.4
  269.0 30.7 reduce-scatter.1
where the time goes:
time: 309 us; the launch traced here: 308 us
  waiting for transfers between devices  164 us (53%)
  local copies, waits for them, and re-layouts  78 us (25%)
  matrix products  30.9 us (10%)
  other arithmetic  14.2 us (5%)
  between operations  13.5 us (4%)
  starting transfers between devices  6.96 us (2%)
    all_gather x1, waiting for transfers between devices, body(): shard_kv = lax.all_gather(prefix_cache, 'req', axis=1, tiled=True)  97 us
    all_gather x1, waiting for transfers between devices, body(): gathered = lax.all_gather(normed_two, 'grp', axis=0, tiled=True)  36.3 us
    reduce_scatter x1, waiting for transfers between devices, body(): lax.psum_scatter(feed_forward(gathered, w_in, w_out).astype(jnp.bfloat16)...  31 us
    unnamed x57, local copies, waits for them, and re-layouts  15.5 us
    slice x3, local copies, waits for them, and re-layouts, body(): value_rows = block[:, :, D:].reshape(-1, H, DK)  15.4 us
    dynamic_slice x3, local copies, waits for them, and re-layouts, body(): rel_terms = lax.dynamic_slice_in_dim(prefix_bias, begin, width, 2)  11 us
    add x2, local copies, waits for them, and re-layouts, body(): prefix_scores + rel_terms[:, :, None, :]  10.6 us
    dot_general x4, matrix products, bias_lookup(): jnp.einsum('qkb,bh->hqk', one_hot, rel_bias, precision=lax.Precision.HIGH...  8.1 us
  transfers between devices with their start and end apart: 5, of which 3 were waited for; matrix products, arithmetic and copies ran while one was open for 17% of the time, Pallas kernels for 0%

commit v1 on v0

--- a/solution.py
+++ b/solution.py
@@ -138,7 +138,8 @@
         jnp.zeros((H, rows_here, DK), jnp.float32),
     )
     running = empty_state
-    shard_kv = lax.all_gather(prefix_cache, "req", axis=1, tiled=True)
+    sent = jnp.stack([prefix_cache] * lax.axis_size("req"))
+    shard_kv = jnp.concatenate(lax.all_to_all(sent, "req", 0, 0), axis=1)
     prefix_ids = jnp.arange(PREF_GRP, dtype=jnp.int32)
     slices = shard_kv.shape[0]
     piece_len = shard_kv.shape[1]

time: 309 us -> 212 us (0.69)
  waiting for transfers between devices: 164 us -> 61.2 us
  starting transfers between devices: 6.96 us -> 18.2 us
  local copies, waits for them, and re-layouts: 78 us -> 72.5 us
    all_gather x1 -> x0, waiting for transfers between devices: 97 us -> none  [body(): shard_kv = lax.all_gather(prefix_cache, 'req', axis=1, tiled=True)]
    all_to_all x0 -> x1, starting transfers between devices: none -> 11.4 us  [body(): shard_kv = jnp.concatenate(lax.all_to_all(sent, 'req', 0, 0), axis=1)]
    all_gather x1, waiting for transfers between devices: 36.3 us -> 25 us  [body(): gathered = lax.all_gather(normed_two, 'grp', axis=0, tiled=True)]
    unnamed x57 -> x56, local copies, waits for them, and re-layouts: 15.5 us -> 6.3 us
    slice x3, local copies, waits for them, and re-layouts: 15.4 us -> 9.44 us  [body(): value_rows = block[:, :, D:].reshape(-1, H, DK)]
    all_to_all x0 -> x1, waiting for transfers between devices: none -> 5.23 us  [body(): shard_kv = jnp.concatenate(lax.all_to_all(sent, 'req', 0, 0), axis=1)]
    slice x0 -> x2, local copies, waits for them, and re-layouts: none -> 4.56 us  [body(): key_rows = block[:, :, :D].reshape(slices, width, H, DK)]
  transfers between devices with their start and end apart: 5 -> 5, of which waited for: 3 -> 3; matrix products, arithmetic and copies ran while one was open for 17% -> 24% of each run, Pallas kernels for 0% -> 0%
where the time goes in v1:
time: 212 us; the launch traced here: 211 us
  local copies, waits for them, and re-layouts  72.5 us (34%)
  waiting for transfers between devices  61.2 us (29%)
  matrix products  31 us (15%)
  starting transfers between devices  18.2 us (9%)
  other arithmetic  14.3 us (7%)
  between operations  13.9 us (7%)
    reduce_scatter x1, waiting for transfers between devices, body(): lax.psum_scatter(feed_forward(gathered, w_in, w_out).astype(jnp.bfloat16)...  31 us
    all_gather x1, waiting for transfers between devices, body(): gathered = lax.all_gather(normed_two, 'grp', axis=0, tiled=True)  25 us
    all_to_all x1, starting transfers between devices, body(): shard_kv = jnp.concatenate(lax.all_to_all(sent, 'req', 0, 0), axis=1)  11.4 us
    dynamic_slice x3, local copies, waits for them, and re-layouts, body(): rel_terms = lax.dynamic_slice_in_dim(prefix_bias, begin, width, 2)  11.1 us
    add x2, local copies, waits for them, and re-layouts, body(): prefix_scores + rel_terms[:, :, None, :]  10.6 us
    slice x3, local copies, waits for them, and re-layouts, body(): value_rows = block[:, :, D:].reshape(-1, H, DK)  9.44 us
    dot_general x4, matrix products, bias_lookup(): jnp.einsum('qkb,bh->hqk', one_hot, rel_bias, precision=lax.Precision.HIGH...  8.14 us
    dot_general x3, local copies, waits for them, and re-layouts, bias_lookup(): jnp.einsum('qkb,bh->hqk', one_hot, rel_bias, precision=lax.Precision.HIGH...  6.53 us
  transfers between devices with their start and end apart: 5, of which 3 were waited for; matrix products, arithmetic and copies ran while one was open for 24% of the time, Pallas kernels for 0%

profile of v1, /device:TPU:1, one launch (start us, length us, event | category | flops | bytes accessed | tf_op | source)
XLA Modules:
  0.0 211.1 jit_solution(5509230421827168940)
XLA Ops:
  6.5 1.2 fusion.46
  7.8 2.2 %convolution_convert_fusion.1 = bf16[128,1024]{1,0:T(8,128)(2,1)S(1)} fusion(bf16[1024,1024]{1,0:T(8,128)(2,1)} %param.17, bf16[128,1024]{1,0:T(8,128)(2,1)} %param.13, f32[1024]{0:T(1024)} %param.14, f32[128]{0:T(128)S(1)} %add_rsqrt_fusion.1), kind=kOutput, calls=%fused_computation.56 | convolution fusion | flops 269090816 | bytes 2626048 | tf_op jit(solution)/shard_map/dot_general | solution.py:127
  10.1 0.5 convolution_convert_fusion.2
  10.8 0.9 pad_maximum_fusion
  11.6 1.3 collective-permute-start.1
  12.9 5.5 %collective-permute-start = (bf16[128,2048]{1,0:T(8,128)(2,1)}, bf16[128,2048]{1,0:T(8,128)(2,1)}, u32[]{:S(2)}, u32[]{:S(2)}) collective-permute-start(bf16[128,2048]{1,0:T(8,128)(2,1)} %pad_maximum_fusion), channel_id=1, source_target_pairs={{0,1},{1,2},{2,3},{3,4},{4,5},{5,6},{6,7},{7,8},{8,9},{9,10},{10,1... | collective-permute-start | bytes 1572872 | tf_op jit(solution)/shard_map/ppermute | solution.py:23
  18.4 2.5 %stack.2 = bf16[32,2,16,2048]{3,2,1,0:T(8,128)(2,1)} broadcast(bf16[2,16,2048]{2,1,0:T(8,128)(2,1)S(1)} %copy-done.21), dimensions={1,2,3} | broadcast | bytes 4325376 | tf_op jit(solution)/shard_map/stack | solution.py:141
  20.9 11.4 %all-to-all-start = ((bf16[32,2,16,2048]{3,2,1,0:T(8,128)(2,1)}), bf16[32,2,16,2048]{3,2,1,0:T(8,128)(2,1)}, u32[]{:S(2)}, u32[]{:S(2)}) async-start(bf16[32,2,16,2048]{3,2,1,0:T(8,128)(2,1)} %stack.2), calls=%async_computation | async-start | bytes 8388608 | tf_op jit(solution)/shard_map/all_to_all | solution.py:142
  32.4 0.8 copy.108
  33.2 2.1 convolution_convert_fusion.3
  36.1 0.9 fusion.90
  36.9 0.7 fusion.12
  37.7 1.4 copy.109
  39.3 0.3 fusion.68
  39.6 2.7 %fusion.13 = f32[128,128,16]{1,2,0:T(8,128)} fusion(s32[128,128]{1,0:T(8,128)} %get-tuple-element.57, f32[32,16]{0,1:T(8,128)S(1)} %copy-done.20), kind=kOutput, calls=%fused_computation.26 | convolution fusion | flops 101187584 | bytes 1116160 | tf_op jit(solution)/shard_map/qkb,bh->hqk/dot_general | solution.py:40
  42.2 1.3 fusion.137
  43.6 3.0 %fusion.10 = f32[16,128,512]{2,0,1:T(8,128)S(1)} fusion(s32[128,512]{1,0:T(8,128)S(1)} %fusion.68, f32[32,16]{0,1:T(8,128)S(1)} %copy-done.20), kind=kOutput, calls=%fused_computation.17 | convolution fusion | flops 404750336 | bytes 4458496 | tf_op jit(solution)/shard_map/qkb,bh->hqk/dot_general | solution.py:40
  46.6 2.7 %fusion.131 = (f32[16,128,256]{2,0,1:T(8,128)}, f32[16,128,256]{2,0,1:T(8,128)}) fusion(f32[16,128,512]{2,0,1:T(8,128)S(1)} %fusion.10), kind=kLoop, calls=%fused_computation.204 | loop fusion | bytes 8388608 | tf_op jit(solution)/shard_map/dynamic_slice | solution.py:152
  49.2 1.7 fusion.11
  51.2 1.8 copy.110
  53.0 2.6 %copy.113 = f32[128,128,16]{0,1,2:T(8,128)} copy(f32[128,128,16]{1,2,0:T(8,128)} %fusion.13) | data formatting | bytes 2097152 | tf_op jit(solution)/shard_map/qkb,bh->hqk/dot_general | solution.py:40
  55.6 4.2 %copy.94 = f32[16,128,256]{2,1,0:T(8,128)} copy(f32[16,128,256]{2,0,1:T(8,128)} %get-tuple-element.28) | data formatting | bytes 4194304 | tf_op jit(solution)/shard_map/dynamic_slice | solution.py:152
  59.8 2.6 %copy.105 = f32[128,128,16]{0,1,2:T(8,128)} copy(f32[128,128,16]{1,2,0:T(8,128)} %fusion.11) | data formatting | bytes 2097152 | tf_op jit(solution)/shard_map/qkb,bh->hqk/dot_general | solution.py:40
  62.3 4.2 %copy.100 = f32[16,128,256]{2,1,0:T(8,128)} copy(f32[16,128,256]{2,0,1:T(8,128)} %get-tuple-element.29) | data formatting | bytes 4194304 | tf_op jit(solution)/shard_map/dynamic_slice | solution.py:152
  66.5 1.9 fusion.133
  68.4 1.8 copy.114
  70.2 1.8 copy.112
  72.0 1.9 fusion.132
  73.8 1.8 copy.104
  75.6 1.8 copy.106
  77.4 2.0 fusion.136
  79.4 1.0 copy-done.3
  80.6 0.4 fusion.138
  81.0 1.0 copy-done.7
  82.2 5.2 %all-to-all-done = bf16[32,2,16,2048]{3,2,1,0:T(8,128)(2,1)} async-done(((bf16[32,2,16,2048]{3,2,1,0:T(8,128)(2,1)}), bf16[32,2,16,2048]{3,2,1,0:T(8,128)(2,1)}, u32[]{:S(2)}, u32[]{:S(2)}) %all-to-all-start) | async-done | bytes 4194336 | tf_op jit(solution)/shard_map/all_to_all | solution.py:142
  87.4 2.5 %copy.91 = bf16[32,2,16,2048]{3,2,0,1:T(8,128)(2,1)S(1)} copy(bf16[32,2,16,2048]{3,2,1,0:T(8,128)(2,1)} %all-to-all-done) | data formatting | bytes 8388608 | tf_op jit(solution)/shard_map/all_to_all | solution.py:142
  89.9 2.1 %fusion.130 = (bf16[2,256,1024]{2,1,0:T(8,128)(2,1)}, bf16[2,256,1024]{2,1,0:T(8,128)(2,1)}, bf16[2,256,1024]{2,1,0:T(8,128)(2,1)}, bf16[2,256,1024]{2,1,0:T(8,128)(2,1)}) fusion(bf16[2,512,2048]{2,1,0:T(8,128)(2,1)S(1)} %bitcast.213), kind=kLoop, calls=%fused_computation.203 | loop fusion | bytes 8388608 | tf_op jit(solution)/shard_map/slice | solution.py:151
  92.0 2.3 %copy.92 = bf16[2,256,1024]{1,2,0:T(8,128)(2,1)} copy(bf16[2,256,1024]{2,1,0:T(8,128)(2,1)} %get-tuple-element.27) | data formatting | bytes 2097152 | tf_op jit(solution)/shard_map/slice | solution.py:150
  94.3 2.3 %copy.98 = bf16[2,256,1024]{1,2,0:T(8,128)(2,1)} copy(bf16[2,256,1024]{2,1,0:T(8,128)(2,1)} %get-tuple-element.25) | data formatting | bytes 2097152 | tf_op jit(solution)/shard_map/slice | solution.py:150
  96.6 2.9 %select_reduce_fusion.3 = (f32[16,128]{1,0:T(8,128)S(1)}, f32[16,128,2,256]{3,1,2,0:T(8,128)S(1)}) fusion(pred[128,2]{0,1:T(4,128)(4,1)S(1)} %iota_compare_fusion.10, f32[16,128,256]{2,1,0:T(8,128)} %copy.94, bf16[128,16,64,1]{0,2,3,1:T(8,128)(2,1)S(1)} %bitcast.217, bf16[2,256,16,64]{1,3,2,0:T(8,128)(2,1)} %bitcast.219), kind=kOutput, calls=%fused_computation.16 | convolution fusion | flops 137361408 | bytes 7610624 | tf_op jit(solution)/shard_map/qhd,swhd->hqsw/dot_general | solution.py:153
  99.5 2.4 %select_reduce_fusion.1 = (f32[16,128]{1,0:T(8,128)}, f32[16,128]{1,0:T(8,128)S(1)}, f32[16,128,2,256]{3,1,2,0:T(8,128)S(1)}) fusion(f32[16,128,2,256]{3,1,2,0:T(8,128)S(1)} %get-tuple-element.62, f32[16,128]{1,0:T(8,128)S(1)} %get-tuple-element.61, pred[128,2]{0,1:T(4,128)(4,1)S(1)} %iota_compare_fusion.10, f32[16,128,256]{2,1,0:T(8,128)S(1)} %copy-done.15, ...), kind=kOutput, calls=%fused_computation.13 | convolution fusion | flops 141553664 | bytes 11821312 | tf_op jit(solution)/shard_map/qhd,swhd->hqsw/dot_general | solution.py:153
  102.0 2.0 copy-done.2
  103.9 1.2 select_reduce_fusion
  105.2 5.3 %copy.101 = f32[16,128,2,256]{1,3,2,0:T(8,128)} copy(f32[16,128,2,256]{3,1,2,0:T(8,128)} %copy-done.2) | data formatting | bytes 8388608 | tf_op jit(solution)/shard_map/add | solution.py:156
  110.5 5.3 %copy.95 = f32[16,128,2,256]{1,3,2,0:T(8,128)} copy(f32[16,128,2,256]{3,1,2,0:T(8,128)} %copy-done.1) | data formatting | bytes 8388608 | tf_op jit(solution)/shard_map/add | solution.py:156
  115.8 3.7 %copy.96 = bf16[2,256,1024]{1,0,2:T(2,128)(2,1)} copy(bf16[2,256,1024]{2,1,0:T(8,128)(2,1)} %get-tuple-element.26) | data formatting | bytes 2097152 | tf_op jit(solution)/shard_map/slice | solution.py:151
  119.5 2.6 %reshape.546 = bf16[512,16,64]{0,2,1:T(8,128)(2,1)} reshape(bf16[2,256,1024]{1,0,2:T(2,128)(2,1)} %copy.96) | data formatting | bytes 2097152 | tf_op jit(solution)/shard_map/reshape | solution.py:151
  122.1 3.7 %copy.102 = bf16[2,256,1024]{1,0,2:T(2,128)(2,1)} copy(bf16[2,256,1024]{2,1,0:T(8,128)(2,1)} %get-tuple-element.24) | data formatting | bytes 2097152 | tf_op jit(solution)/shard_map/slice | solution.py:151
  125.7 2.6 %reshape.549 = bf16[512,16,64]{0,2,1:T(8,128)(2,1)} reshape(bf16[2,256,1024]{1,0,2:T(2,128)(2,1)} %copy.102) | data formatting | bytes 2097152 | tf_op jit(solution)/shard_map/reshape | solution.py:151
  128.3 0.7 fusion.94
  129.0 1.6 fusion.31
  130.9 5.3 %fusion.4 = (bf16[16,128,512]{1,2,0:T(8,128)(2,1)S(1)}, bf16[16,128,512]{1,2,0:T(8,128)(2,1)S(1)}) fusion(f32[16,128,2,256]{1,3,2,0:T(8,128)} %copy.101, f32[16,128]{1,0:T(8,128)S(1)} %get-tuple-element.12, pred[128,512]{0,1:T(8,128)(4,1)S(1)} %bitcast.226, f32[16,128]{1,0:T(8,128)S(1)} %get-tuple-element.61, f32[16,128,2,256]{1,3,2,0:T(8,128)} %copy.95), kind=kLoop, calls=%fused_computation.6 | loop fusion | flops 8388608 | bytes 12664832 | tf_op jit(solution)/shard_map/convert_element_type | solution.py:75
  136.3 0.5 fusion.21
  136.8 0.7 copy-done.11
  137.5 0.5 fusion.22
  138.1 0.7 copy-done.8
  138.8 0.3 fusion.32
  139.1 0.7 copy-done.14
  139.8 0.5 multiply_reduce_fusion
  140.4 0.8 multiply_convert_fusion
  141.3 25.0 %all-gather.2.cloned.1.call-done = bf16[512,1024]{1,0:T(8,128)(2,1)} async-done(((bf16[128,1024]{1,0:T(8,128)(2,1)}), bf16[512,1024]{1,0:T(8,128)(2,1)}) %all-gather.2.cloned.1.call-update) | async-done | bytes 1048592 | tf_op jit(solution)/shard_map/all_gather | solution.py:193
  166.3 5.3 %convolution_convert_fusion = bf16[512,1024]{1,0:T(8,128)(2,1)} fusion(bf16[1024,1024]{1,0:T(8,128)(2,1)S(1)} %copy-done, bf16[512,1024]{1,0:T(8,128)(2,1)} %all-gather.2.cloned.1.call-done, bf16[1024,1024]{1,0:T(8,128)(2,1)} %param.24), kind=kOutput, calls=%fused_computation.27 | convolution fusion | flops 2149056512 | bytes 6291456 | tf_op jit(solution)/shard_map/dot_general | solution.py:96
  171.6 31.0 %reduce-scatter.2.cloned.1.call-done = bf16[128,1024]{1,0:T(8,128)(2,1)} async-done(((bf16[512,1024]{1,0:T(8,128)(2,1)}), bf16[128,1024]{1,0:T(8,128)(2,1)}) %reduce-scatter.2.cloned.1.call-update) | async-done | bytes 262160 | tf_op jit(solution)/shard_map/reduce_scatter | solution.py:194
  202.5 1.7 add_convert_fusion
  (80 shorter events, 2.2 us)
Async XLA Ops:
  6.5 159.8 %copy-start = (bf16[1024,1024]{1,0:T(8,128)(2,1)S(1)}, bf16[1024,1024]{1,0:T(8,128)(2,1)}, u32[]{:S(2)}) copy-start(bf16[1024,1024]{1,0:T(8,128)(2,1)} %param.25) | copy-start | bytes 6291460
  6.5 3.5 %copy-start.4 = (bf16[128,1024]{1,0:T(8,128)(2,1)S(1)}, bf16[128,1024]{1,0:T(8,128)(2,1)}, u32[]{:S(2)}) copy-start(bf16[128,1024]{1,0:T(8,128)(2,1)} %param.13) | copy-start | bytes 786436
  6.5 3.5 %copy-start.22 = (f32[1024]{0:T(1024)S(1)}, f32[1024]{0:T(1024)}, u32[]{:S(2)}) copy-start(f32[1024]{0:T(1024)} %param.14) | copy-start | bytes 12292
  6.5 3.5 %copy-start.13 = (bf16[1024,1024]{1,0:T(8,128)(2,1)S(1)}, bf16[1024,1024]{1,0:T(8,128)(2,1)}, u32[]{:S(2)}) copy-start(bf16[1024,1024]{1,0:T(8,128)(2,1)} %param.16) | copy-start | bytes 6291460
  10.1 0.7 copy-start.12
  10.1 8.3 %copy-start.21 = (bf16[2,16,2048]{2,1,0:T(8,128)(2,1)S(1)}, bf16[2,16,2048]{2,1,0:T(8,128)(2,1)}, u32[]{:S(2)}) copy-start(bf16[2,16,2048]{2,1,0:T(8,128)(2,1)} %param.20) | copy-start | bytes 393220
  11.6 54.9 %collective-permute-start.1 = (bf16[128,2048]{1,0:T(8,128)(2,1)}, bf16[128,2048]{1,0:T(8,128)(2,1)}, u32[]{:S(2)}, u32[]{:S(2)}) collective-permute-start(bf16[128,2048]{1,0:T(8,128)(2,1)} %pad_maximum_fusion), channel_id=1, source_target_pairs={{1,0},{2,1},{3,2},{4,3},{5,4},{6,5},{7,6},{8,7},{9,8},{10,9},{11,1... | collective-permute-start | bytes 1572872 | tf_op jit(solution)/shard_map/ppermute | solution.py:24
  12.9 59.0 %collective-permute-start = (bf16[128,2048]{1,0:T(8,128)(2,1)}, bf16[128,2048]{1,0:T(8,128)(2,1)}, u32[]{:S(2)}, u32[]{:S(2)}) collective-permute-start(bf16[128,2048]{1,0:T(8,128)(2,1)} %pad_maximum_fusion), channel_id=1, source_target_pairs={{0,1},{1,2},{2,3},{3,4},{4,5},{5,6},{6,7},{7,8},{8,9},{9,10},{10,1... | collective-permute-start | bytes 1572872 | tf_op jit(solution)/shard_map/ppermute | solution.py:23
  20.9 66.5 %all-to-all-start = ((bf16[32,2,16,2048]{3,2,1,0:T(8,128)(2,1)}), bf16[32,2,16,2048]{3,2,1,0:T(8,128)(2,1)}, u32[]{:S(2)}, u32[]{:S(2)}) async-start(bf16[32,2,16,2048]{3,2,1,0:T(8,128)(2,1)} %stack.2), calls=%async_computation | async-start | bytes 8388608 | tf_op jit(solution)/shard_map/all_to_all | solution.py:142
  32.3 3.2 %copy-start.26 = (s32[1,64]{1,0:T(1,128)S(1)}, s32[1,64]{1,0:T(1,128)}, u32[]{:S(2)}) copy-start(s32[1,64]{1,0:T(1,128)} %param.21) | copy-start | bytes 772
  32.3 3.6 %copy-start.27 = (s32[1,64]{1,0:T(1,128)S(1)}, s32[1,64]{1,0:T(1,128)}, u32[]{:S(2)}) copy-start(s32[1,64]{1,0:T(1,128)} %param.22) | copy-start | bytes 772
  32.3 4.6 %copy-start.20 = (f32[32,16]{0,1:T(8,128)S(1)}, f32[32,16]{0,1:T(8,128)}, u32[]{:S(2)}) copy-start(f32[32,16]{0,1:T(8,128)} %param.19) | copy-start | bytes 6148
  32.3 134.0 %all-gather.2.cloned.1.call-start = ((), (), s32[]{:S(2)}) async-start(), calls=%async_computation.2 | async-start | bytes 1310720 | tf_op jit(solution)/shard_map/all_gather | solution.py:193
  39.1 3.2 %copy-start.10 = (f32[128,128,16]{0,1,2:T(8,128)S(1)}, f32[128,128,16]{0,1,2:T(8,128)}, u32[]{:S(2)}) copy-start(f32[128,128,16]{0,1,2:T(8,128)} %copy.109) | copy-start | bytes 3145732
  66.5 35.5 %copy-start.23 = (pred[128,2]{0,1:T(4,128)(4,1)}, pred[128,2]{0,1:T(4,128)(4,1)S(1)}, u32[]{:S(2)}) copy-start(pred[128,2]{0,1:T(4,128)(4,1)S(1)} %iota_compare_fusion.10) | copy-start | bytes 772
  77.4 3.2 %copy-start.9 = (f32[128,128,16]{0,1,2:T(8,128)S(1)}, f32[128,128,16]{0,1,2:T(8,128)}, u32[]{:S(2)}) copy-start(f32[128,128,16]{0,1,2:T(8,128)} %copy.105) | copy-start | bytes 3145732
  77.4 3.2 %copy-start.17 = (bf16[128,1024]{0,1:T(8,128)(2,1)S(1)}, bf16[128,1024]{0,1:T(8,128)(2,1)}, u32[]{:S(2)}) copy-start(bf16[128,1024]{0,1:T(8,128)(2,1)} %copy.104) | copy-start | bytes 786436
  79.4 1.0 copy-start.3
  81.0 1.0 copy-start.7
  96.6 2.9 %copy-start.15 = (f32[16,128,256]{2,1,0:T(8,128)S(1)}, f32[16,128,256]{2,1,0:T(8,128)}, u32[]{:S(2)}) copy-start(f32[16,128,256]{2,1,0:T(8,128)} %copy.100) | copy-start | bytes 6291460
  96.6 2.9 %copy-start.18 = (bf16[2,256,1024]{1,2,0:T(8,128)(2,1)S(1)}, bf16[2,256,1024]{1,2,0:T(8,128)(2,1)}, u32[]{:S(2)}) copy-start(bf16[2,256,1024]{1,2,0:T(8,128)(2,1)} %copy.98) | copy-start | bytes 3145732
  99.5 2.5 %copy-start.1 = (f32[16,128,2,256]{3,1,2,0:T(8,128)}, f32[16,128,2,256]{3,1,2,0:T(8,128)S(1)}, u32[]{:S(2)}) copy-start(f32[16,128,2,256]{3,1,2,0:T(8,128)S(1)} %get-tuple-element.62) | copy-start | bytes 12582916
  102.0 2.0 copy-start.2
  125.7 4.9 %copy-start.16 = (bf16[128,1024]{0,1:T(8,128)(2,1)S(1)}, bf16[128,1024]{0,1:T(8,128)(2,1)}, u32[]{:S(2)}) copy-start(bf16[128,1024]{0,1:T(8,128)(2,1)} %copy.110) | copy-start | bytes 786436
  128.3 2.6 %copy-start.24 = (pred[128,2]{0,1:T(4,128)(4,1)S(1)}, pred[128,2]{0,1:T(4,128)(4,1)}, u32[]{:S(2)}) copy-start(pred[128,2]{0,1:T(4,128)(4,1)} %copy-done.23) | copy-start | bytes 772
  130.9 5.4 %copy-start.6 = (bf16[512,16,64]{0,2,1:T(8,128)(2,1)S(1)}, bf16[512,16,64]{0,2,1:T(8,128)(2,1)}, u32[]{:S(2)}) copy-start(bf16[512,16,64]{0,2,1:T(8,128)(2,1)} %reshape.546) | copy-start | bytes 3145732
  136.3 1.2 copy-start.11
  137.5 1.2 copy-start.8
  137.5 1.3 copy-start.19
  138.1 1.1 copy-start.5
  138.1 1.8 copy-start.14
  139.1 1.3 copy-start.25
  141.2 61.3 %reduce-scatter.2.cloned.1.call-start = ((), (), s32[]{:S(2)}) async-start(), calls=%async_computation.3 | async-start | bytes 1310720 | tf_op jit(solution)/shard_map/reduce_scatter | solution.py:194
Sparse Core Ops, SparseCore 0:
  141.4 24.8 all-gather.1
  171.7 30.7 reduce-scatter.1
